TPU v7x, 512 devices: a whole 4x8x8 slice. The times are simulated.
512 devices in a mesh: lon: 64 (over z_lo, x, y), lat: 8 (over z_hi, core).
Axes of the slice: x: 4, y: 8, z: 8 (z_hi: 4, z_lo: 2; z = z_hi * 2 + z_lo), core: 2. Of those that a mesh axis runs over, the one named last changes fastest.
Arguments:
- thermal_anomaly: float32 [16, 512, 1024], P(None, 'lon', 'lat'), may hold values from -6 to 6
- saltiness_anomaly: float32 [16, 512, 1024], P(None, 'lon', 'lat'), may hold values from -6 to 6
- zonal_current: float32 [16, 512, 1024], P(None, 'lon', 'lat'), may hold values from -3 to 3
- meridional_current: float32 [16, 512, 1024], P(None, 'lon', 'lat'), may hold values from -3 to 3
- bottom_ocean_layer: int32 [512, 1024], P('lon', 'lat'), may hold values from 0 to 16
- seam_axis_meridian: int32 [1], replicated, may hold values from 0 to 1023
- interface_diffusivity: float32 [15, 512, 1024], P(None, 'lon', 'lat'), may hold values from 0.1 to 10
- atmospheric_forcing: float32 [2, 512, 1024], P(None, 'lon', 'lat'), may hold values from -6 to 6
Outputs:
- temperature_next: float32 [16, 512, 1024], P(None, 'lon', 'lat')
- salinity_next: float32 [16, 512, 1024], P(None, 'lon', 'lat')
- zonal_next: float32 [16, 512, 1024], P(None, 'lon', 'lat')
- meridional_next: float32 [16, 512, 1024], P(None, 'lon', 'lat')
Inputs may be any that keep to these rules, and one draw needn't show every extreme that they name: `seam_axis_meridian`: an even code folds about a cell centre, an odd one about a cell corner.
All inputs are finite; a program needn't handle non-finite values.
Results may differ from a plain program's by a relative error of at most 0.0003.
Values sent between devices are 32-bit elements; how exact they have to be, the bound alone decides.
A program may use at most 64 MiB of HBM per device.

v0:
```python
import jax
import jax.numpy as jnp
from jax import lax
from jax.sharding import PartitionSpec as P

TIME_STEP = 0.2
TRACER_DIFF = 0.2
MOMENTUM_VISC = 0.2
THERMAL_EXPANSION = 0.5
HALINE_CONTRACTION = 0.4
WIND_GAIN = 2.0
VERTICAL_VISC = 1.0
NEIGHBOURS = ((1, 0), (-1, 0), (0, 1), (0, -1))


def padded(block, sides, width):
    for axis, dim in sides:
        count = lax.axis_size(axis)
        forward = [(i, i + 1) for i in range(count - 1)]
        forward.append((count - 1, 0))
        backward = [(target, source) for source, target in forward]
        low = lax.ppermute(
            lax.slice_in_dim(block, block.shape[dim] - width, None, axis=dim), axis, forward
        )
        high = lax.ppermute(lax.slice_in_dim(block, 0, width, axis=dim), axis, backward)
        block = jnp.concatenate([low, block, high], axis=dim)
    return block


def implicit(right_side, coupling):
    count = right_side.shape[-3]
    ratios = []
    values = []
    for level_k in range(count):
        below = coupling[level_k] if level_k < count - 1 else 0.0
        above = coupling[level_k - 1] if level_k > 0 else 0.0
        if level_k == 0:
            denom = 1.0 + below
            values.append(right_side[..., 0, :, :] / denom)
        else:
            denom = 1.0 + above + below + above * ratios[level_k - 1]
            values.append((right_side[..., level_k, :, :] + above * values[level_k - 1]) / denom)
        ratios.append(-below / denom)
    result = [values[count - 1]]
    for level_k in range(count - 2, -1, -1):
        result.insert(0, values[level_k] - ratios[level_k] * result[0])
    return jnp.stack(result, axis=-3)


def choose_rows(source, fold_type, sign_column):
    upper = jnp.where(fold_type == 1, source[..., 2], source[..., 1])
    outer = jnp.where(fold_type == 1, source[..., 1], source[..., 0])
    return jnp.stack([upper, outer], axis=-1) * sign_column


def advance(grid_ext, interface_diffusivity, atmospheric_forcing, row_start, rows_total):
    layer_number = (grid_ext.shape[0] - 1) // 4
    cols_n = grid_ext.shape[1] - 4
    rows_n = grid_ext.shape[2] - 4

    def view(source_array, shift_x, shift_y):
        return source_array[
            ..., 2 + shift_x : 2 + shift_x + cols_n, 2 + shift_y : 2 + shift_y + rows_n
        ]

    tracers = grid_ext[: 2 * layer_number].reshape(2, layer_number, cols_n + 4, rows_n + 4)
    zonal = grid_ext[2 * layer_number : 3 * layer_number]
    merid = grid_ext[3 * layer_number : 4 * layer_number]
    depth_count = grid_ext[4 * layer_number]
    level_ids = jnp.arange(layer_number).astype(jnp.float32)[:, None, None]
    wet_mask = jnp.where(level_ids < depth_count[None], 1.0, 0.0).astype(jnp.float32)

    def face_x(shift_x):
        interp = (
            7.0 * (view(tracers, shift_x, 0) + view(tracers, shift_x + 1, 0))
            - (view(tracers, shift_x - 1, 0) + view(tracers, shift_x + 2, 0))
        ) / 12.0
        return (
            view(zonal, shift_x, 0)
            * view(wet_mask, shift_x, 0)
            * view(wet_mask, shift_x + 1, 0)
            * interp
        )

    def face_y(shift_y):
        interp = (
            7.0 * (view(tracers, 0, shift_y) + view(tracers, 0, shift_y + 1))
            - (view(tracers, 0, shift_y - 1) + view(tracers, 0, shift_y + 2))
        ) / 12.0
        return (
            view(merid, 0, shift_y)
            * view(wet_mask, 0, shift_y)
            * view(wet_mask, 0, shift_y + 1)
            * interp
        )

    advect = -(face_x(0) - face_x(-1)) - (face_y(0) - face_y(-1))
    centre = view(tracers, 0, 0)
    wet_centre = view(wet_mask, 0, 0)
    spread = jnp.zeros_like(centre)
    for shift_x, shift_y in NEIGHBOURS:
        spread = spread + view(wet_mask, shift_x, shift_y) * wet_centre * (
            view(tracers, shift_x, shift_y) - centre
        )
    tracer_star = centre + TIME_STEP * (advect + TRACER_DIFF * spread) * wet_centre
    buoyancy = (
        THERMAL_EXPANSION * grid_ext[:layer_number]
        - HALINE_CONTRACTION * grid_ext[layer_number : 2 * layer_number]
    ) * wet_mask
    pressure = jnp.cumsum(buoyancy, axis=0) - 0.5 * buoyancy
    u_mask = wet_centre * view(wet_mask, 1, 0)
    v_mask = wet_centre * view(wet_mask, 0, 1)
    row_ids = (row_start + jnp.arange(rows_n)).astype(jnp.float32)
    cor_u = 2.0 * (row_ids + 0.5) / rows_total - 1.0
    cor_v = 2.0 * (row_ids + 1.0) / rows_total - 1.0
    v_at_u = 0.25 * (
        view(merid, 0, 0) + view(merid, 0, -1) + view(merid, 1, 0) + view(merid, 1, -1)
    )
    u_at_v = 0.25 * (
        view(zonal, 0, 0) + view(zonal, -1, 0) + view(zonal, 0, 1) + view(zonal, -1, 1)
    )
    u_centre = view(zonal, 0, 0)
    v_centre = view(merid, 0, 0)
    u_visc = jnp.zeros_like(u_centre)
    v_visc = jnp.zeros_like(v_centre)
    for shift_x, shift_y in NEIGHBOURS:
        u_visc = u_visc + view(wet_mask, shift_x, shift_y) * view(
            wet_mask, shift_x + 1, shift_y
        ) * u_mask * (view(zonal, shift_x, shift_y) - u_centre)
        v_visc = v_visc + view(wet_mask, shift_x, shift_y) * view(
            wet_mask, shift_x, shift_y + 1
        ) * v_mask * (view(merid, shift_x, shift_y) - v_centre)
    u_star = (
        u_centre
        + TIME_STEP
        * (cor_u * v_at_u - (view(pressure, 1, 0) - view(pressure, 0, 0)) + MOMENTUM_VISC * u_visc)
    ) * u_mask
    v_star = (
        v_centre
        + TIME_STEP
        * (-cor_v * u_at_v - (view(pressure, 0, 1) - view(pressure, 0, 0)) + MOMENTUM_VISC * v_visc)
    ) * v_mask
    u_star = u_star.at[0].add(TIME_STEP * WIND_GAIN * atmospheric_forcing[0] * u_mask[0])
    v_star = v_star.at[0].add(TIME_STEP * WIND_GAIN * atmospheric_forcing[1] * v_mask[0])
    tracer_next = implicit(
        tracer_star, TIME_STEP * interface_diffusivity * wet_centre[:-1] * wet_centre[1:]
    )
    u_next = implicit(u_star, TIME_STEP * VERTICAL_VISC * u_mask[:-1] * u_mask[1:])
    v_next = implicit(v_star, TIME_STEP * VERTICAL_VISC * v_mask[:-1] * v_mask[1:])
    return (tracer_next[0], tracer_next[1], u_next, v_next)


def shards(
    thermal_anomaly,
    saltiness_anomaly,
    zonal_current,
    meridional_current,
    bottom_ocean_layer,
    seam_axis_meridian,
    interface_diffusivity,
    atmospheric_forcing,
):
    layer_number = thermal_anomaly.shape[0]
    block_meridian_number = thermal_anomaly.shape[1]
    block_parallel_number = thermal_anomaly.shape[2]
    combined_arrays = jnp.concatenate(
        [
            thermal_anomaly,
            saltiness_anomaly,
            zonal_current,
            meridional_current,
            bottom_ocean_layer.astype(jnp.float32)[None],
        ],
        axis=0,
    )
    lon_count = lax.axis_size("lon")
    lat_count = lax.axis_size("lat")
    lon_index = lax.axis_index("lon")
    lat_index = lax.axis_index("lat")
    total_lon = block_meridian_number * lon_count
    fold_code = seam_axis_meridian[0]
    fold_type = jnp.mod(fold_code, 2)
    sign_column = jnp.concatenate(
        [
            jnp.ones((2 * layer_number,), jnp.float32),
            -jnp.ones((2 * layer_number,), jnp.float32),
            jnp.ones((1,), jnp.float32),
        ]
    )[:, None, None]
    top_rows = combined_arrays[:, :, block_parallel_number - 3 :]
    margin = 2
    first_col = lon_index * block_meridian_number - margin
    col_count = block_meridian_number + 2 * margin
    targets = jnp.mod(fold_code - (first_col + jnp.arange(col_count)), total_lon)
    piece = lax.all_gather(top_rows, "lon", axis=1, tiled=True)
    column_ids = jnp.arange(piece.shape[1])
    selector = jnp.where(column_ids[:, None] == targets[None, :], 1.0, 0.0).astype(jnp.float32)
    source = jnp.einsum("anr,nc->acr", piece, selector, precision=lax.Precision.HIGHEST)
    ghost = choose_rows(source, fold_type, sign_column)
    is_top = lat_index == lat_count - 1
    grid_ext = padded(combined_arrays, (("lon", 1), ("lat", 2)), 2)
    south_keep = jnp.where(
        jnp.logical_and(lat_index == 0, jnp.arange(block_parallel_number + 4) < 2), 0.0, 1.0
    ).astype(jnp.float32)
    grid_ext = grid_ext * south_keep
    grid_ext = jnp.where(
        is_top,
        jnp.concatenate([grid_ext[..., : block_parallel_number + 2], ghost], axis=2),
        grid_ext,
    )
    return advance(
        grid_ext,
        interface_diffusivity,
        atmospheric_forcing,
        lat_index * block_parallel_number,
        block_parallel_number * lat_count,
    )


def solution(mesh):
    placed = (
        P(None, "lon", "lat"),
        P(None, "lon", "lat"),
        P(None, "lon", "lat"),
        P(None, "lon", "lat"),
        P("lon", "lat"),
        P(),
        P(None, "lon", "lat"),
        P(None, "lon", "lat"),
    )
    return jax.shard_map(
        shards,
        mesh=mesh,
        in_specs=placed,
        out_specs=(
            P(None, "lon", "lat"),
            P(None, "lon", "lat"),
            P(None, "lon", "lat"),
            P(None, "lon", "lat"),
        ),
        check_vma=False,
    )
```

profile of v0, /device:TPU:201, one launch (start us, length us, event | category | flops | bytes accessed | tf_op | source)
XLA Modules:
  0.0 341.6 jit_solution(17473160580814597958)
XLA Ops:
  0.6 0.8 constant_dynamic-update-slice_fusion.4
  1.5 0.8 constant_dynamic-update-slice_fusion.3
  2.3 0.8 constant_dynamic-update-slice_fusion.2
  3.2 0.8 constant_dynamic-update-slice_fusion.1
  4.0 0.7 constant_dynamic-update-slice_fusion
  4.7 3.2 collective-permute-start
  8.0 2.1 collective-permute-start.1
  10.7 0.1 slice.759
  10.9 266.5 %all_gather.3 = f32[65,512,3]{2,1,0:T(8,128)} all-gather(f32[65,8,3]{2,1,0:T(8,128)S(1)} %slice.759), channel_id=1, replica_groups=mesh['lon'=64,'lat'=8] {'lon'}, dimensions={1}, use_global_device_ids=true | all-gather | bytes 405600 | tf_op jit(solution)/shard_map/all_gather | solution.py:195
  277.4 0.0 copy-start.3
  277.4 10.2 %copy.565 = f32[65,512,3]{0,1,2:T(8,128)S(1)} copy(f32[65,512,3]{2,1,0:T(8,128)} %all_gather.3) | data formatting | bytes 798720 | tf_op jit(solution)/shard_map/all_gather | solution.py:195
  287.6 0.5 convolution_bitcast_fusion
  288.1 0.0 copy-done.3
  288.2 0.0 collective-permute-done
  288.2 0.0 collective-permute-done.1
  288.2 0.1 pad_maximum_fusion
  288.3 0.2 fusion.166
  288.5 0.2 copy.561
  288.8 38.1 %collective-permute-start.2 = (f32[65,12,2]{0,2,1:T(2,128)S(1)}, f32[65,12,2]{0,2,1:T(2,128)S(1)}, u32[]{:S(2)}, u32[]{:S(2)}) collective-permute-start(f32[65,12,2]{0,2,1:T(2,128)S(1)} %copy.561), channel_id=1, source_target_pairs={{0,1},{1,2},{2,3},{3,4},{4,5},{5,6},{6,7},{7,0},{8,9},{9,10},{10,1... | collective-permute-start | bytes 18728 | tf_op jit(solution)/shard_map/ppermute | solution.py:22
  326.9 0.2 copy.562
  327.1 1.9 collective-permute-start.3
  329.0 0.3 copy.569
  329.4 0.0 collective-permute-done.2
  329.4 0.3 copy.563
  329.7 4.5 %collective-permute-done.3 = f32[65,12,2]{0,2,1:T(2,128)S(1)} collective-permute-done((f32[65,12,2]{0,2,1:T(2,128)S(1)}, f32[65,12,2]{0,2,1:T(2,128)S(1)}, u32[]{:S(2)}, u32[]{:S(2)}) %collective-permute-start.3) | collective-permute-done | bytes 6272 | tf_op jit(solution)/shard_map/ppermute | solution.py:25
  334.2 0.3 copy.564
  334.6 0.8 maximum_multiply_fusion
  335.3 0.3 maximum_select_fusion
  335.6 0.0 copy-start
  335.7 0.2 reduce-window_subtract_fusion
  335.8 0.1 compare_select_fusion
  335.9 0.4 fusion.40
  336.4 0.4 fusion.27
  336.8 0.0 copy-start.2
  336.8 0.2 multiply_multiply_fusion.3
  337.0 0.0 copy-done
  337.0 0.0 copy-start.1
  337.1 0.4 copy-done.2
  337.5 0.1 fusion.70
  337.6 0.1 constant_dynamic-update-slice_fusion.36
  337.8 0.0 copy-start.4
  337.9 0.1 fusion.87
  338.0 0.0 slice-start
  338.0 0.1 constant_dynamic-update-slice_fusion.20
  338.3 0.0 copy-done.1
  338.3 0.0 copy-start.5
  338.3 0.1 slice_multiply_fusion.10
  338.8 0.0 copy-done.4
  338.8 0.2 slice-done
  339.0 0.2 copy.570
  339.3 0.0 copy-done.5
  339.3 0.4 fusion.9
  339.7 0.2 fusion.54
  339.9 0.2 multiply_subtract_fusion
  340.1 0.2 stack.9
  340.3 0.7 copy.582
  341.0 0.7 copy.583
  (67 shorter events, 0.6 us)
Async XLA Ops:
  4.7 283.5 %collective-permute-start = (f32[65,2,128]{2,1,0:T(2,128)S(1)}, f32[65,2,128]{2,1,0:T(2,128)S(1)}, u32[]{:S(2)}, u32[]{:S(2)}) collective-permute-start(f32[65,2,128]{2,1,0:T(2,128)S(1)} %get-tuple-element.201), channel_id=1, source_target_pairs={{0,8},{8,16},{16,24},{24,32},{32,40},{40,48},{48,56},{56,64},{64,7... | collective-permute-start | bytes 199688 | tf_op jit(solution)/shard_map/ppermute | solution.py:22
  8.0 280.2 %collective-permute-start.1 = (f32[65,2,128]{2,1,0:T(2,128)S(1)}, f32[65,2,128]{2,1,0:T(2,128)S(1)}, u32[]{:S(2)}, u32[]{:S(2)}) collective-permute-start(f32[65,2,128]{2,1,0:T(2,128)S(1)} %get-tuple-element.202), channel_id=1, source_target_pairs={{8,0},{16,8},{24,16},{32,24},{40,32},{48,40},{56,48},{64,56},{72,6... | collective-permute-start | bytes 199688 | tf_op jit(solution)/shard_map/ppermute | solution.py:25
  277.4 10.8 %copy-start.3 = (f32[65]{0:T(128)S(1)}, f32[65]{0:T(128)}, u32[]{:S(2)}) copy-start(f32[65]{0:T(128)} %constant.125.clone.1) | copy-start | bytes 784
  288.8 40.6 %collective-permute-start.2 = (f32[65,12,2]{0,2,1:T(2,128)S(1)}, f32[65,12,2]{0,2,1:T(2,128)S(1)}, u32[]{:S(2)}, u32[]{:S(2)}) collective-permute-start(f32[65,12,2]{0,2,1:T(2,128)S(1)} %copy.561), channel_id=1, source_target_pairs={{0,1},{1,2},{2,3},{3,4},{4,5},{5,6},{6,7},{7,0},{8,9},{9,10},{10,1... | collective-permute-start | bytes 18728 | tf_op jit(solution)/shard_map/ppermute | solution.py:22
  327.1 7.1 %collective-permute-start.3 = (f32[65,12,2]{0,2,1:T(2,128)S(1)}, f32[65,12,2]{0,2,1:T(2,128)S(1)}, u32[]{:S(2)}, u32[]{:S(2)}) collective-permute-start(f32[65,12,2]{0,2,1:T(2,128)S(1)} %copy.562), channel_id=1, source_target_pairs={{1,0},{2,1},{3,2},{4,3},{5,4},{6,5},{7,6},{0,7},{9,8},{10,9},{11,1... | collective-permute-start | bytes 18728 | tf_op jit(solution)/shard_map/ppermute | solution.py:25
  335.6 1.4 copy-start
  336.8 0.7 copy-start.2
  337.0 1.2 copy-start.1
  337.8 1.0 copy-start.4
  338.0 1.1 slice-start
  338.3 1.0 copy-start.5
where the time goes:
time: 342 us
  blocking collectives  267 us (78%)
  starting transfers between devices  45.3 us (13%)
  local copies, waits for them, and re-layouts  18.1 us (5%)
  other arithmetic  4.76 us (1%)
  waiting for transfers between devices  4.49 us (1%)
    all_gather x1, blocking collectives, shards(): piece = lax.all_gather(top_rows, 'lon', axis=1, tiled=True)  267 us
    ppermute x2, starting transfers between devices, padded(): lax.ppermute(lax.slice_in_dim(block, block.shape[dim] - width, None, axis...  41.3 us
    all_gather x1, local copies, waits for them, and re-layouts, shards(): piece = lax.all_gather(top_rows, 'lon', axis=1, tiled=True)  10.2 us
  transfers between devices with their start and end apart: 4, of which 1 were waited for; matrix products, arithmetic and copies ran while one was open for 3% of the time, Pallas kernels for 0%

commit v1 on v0

--- a/solution.py
+++ b/solution.py
@@ -192,7 +192,9 @@
     first_col = lon_index * block_meridian_number - margin
     col_count = block_meridian_number + 2 * margin
     targets = jnp.mod(fold_code - (first_col + jnp.arange(col_count)), total_lon)
-    piece = lax.all_gather(top_rows, "lon", axis=1, tiled=True)
+    piece = jnp.concatenate(
+        lax.all_to_all(jnp.stack([top_rows] * lax.axis_size("lon")), "lon", 0, 0), axis=1
+    )
     column_ids = jnp.arange(piece.shape[1])
     selector = jnp.where(column_ids[:, None] == targets[None, :], 1.0, 0.0).astype(jnp.float32)
     source = jnp.einsum("anr,nc->acr", piece, selector, precision=lax.Precision.HIGHEST)

time: 342 us -> 55.8 us (0.16)
  the two profiles are of different devices: /device:TPU:201 before, /device:TPU:128 now
where the time goes in v1:
time: 55.8 us; the launch traced here: 55.2 us
  starting transfers between devices  23.8 us (43%)
  waiting for transfers between devices  16.3 us (29%)
  local copies, waits for them, and re-layouts  8.22 us (15%)
  other arithmetic  4.43 us (8%)
  between operations  2.02 us (4%)
    all_to_all x1, waiting for transfers between devices, shards(): lax.all_to_all(jnp.stack([top_rows] * lax.axis_size('lon')), 'lon', 0, 0)  12.8 us
    ppermute x2, starting transfers between devices, padded(): lax.ppermute(lax.slice_in_dim(block, 0, width, axis=dim), axis, backward)  9.73 us
    all_to_all x1, starting transfers between devices, shards(): lax.all_to_all(jnp.stack([top_rows] * lax.axis_size('lon')), 'lon', 0, 0)  8.13 us
    ppermute x2, starting transfers between devices, padded(): lax.ppermute(lax.slice_in_dim(block, block.shape[dim] - width, None, axis...  5.89 us
    unnamed x37, local copies, waits for them, and re-layouts  4.57 us
    ppermute x2, waiting for transfers between devices, padded(): lax.ppermute(lax.slice_in_dim(block, block.shape[dim] - width, None, axis...  3.49 us
  transfers between devices with their start and end apart: 5, of which 2 were waited for; matrix products, arithmetic and copies ran while one was open for 6% of the time, Pallas kernels for 0%

profile of v1, /device:TPU:128, one launch (start us, length us, event | category | flops | bytes accessed | tf_op | source)
XLA Modules:
  0.0 55.2 jit_solution(7991426174527265181)
XLA Ops:
  0.6 0.8 %constant_dynamic-update-slice_fusion.4 = f32[65,8,128]{2,1,0:T(8,128)S(1)} fusion(f32[16,8,128]{2,1,0:T(8,128)} %param.12), kind=kLoop, calls=%fused_computation.37 | loop fusion | bytes 131072
  1.5 0.8 %constant_dynamic-update-slice_fusion.3 = f32[65,8,128]{2,1,0:T(8,128)S(1)} fusion(f32[65,8,128]{2,1,0:T(8,128)S(1)} %constant_dynamic-update-slice_fusion.4, f32[16,8,128]{2,1,0:T(8,128)} %param.13), kind=kLoop, calls=%fused_computation.36 | loop fusion | bytes 131072
  2.3 0.8 %constant_dynamic-update-slice_fusion.2 = f32[65,8,128]{2,1,0:T(8,128)S(1)} fusion(f32[65,8,128]{2,1,0:T(8,128)S(1)} %constant_dynamic-update-slice_fusion.3, f32[16,8,128]{2,1,0:T(8,128)} %param.14), kind=kLoop, calls=%fused_computation.35 | loop fusion | bytes 131072
  3.2 0.8 %constant_dynamic-update-slice_fusion.1 = f32[65,8,128]{2,1,0:T(8,128)S(1)} fusion(f32[65,8,128]{2,1,0:T(8,128)S(1)} %constant_dynamic-update-slice_fusion.2, f32[16,8,128]{2,1,0:T(8,128)} %param.15), kind=kLoop, calls=%fused_computation.34 | loop fusion | bytes 131072
  4.0 0.7 %constant_dynamic-update-slice_fusion = f32[65,8,128]{2,1,0:T(8,128)S(1)} fusion(f32[65,8,128]{2,1,0:T(8,128)S(1)} %constant_dynamic-update-slice_fusion.1, s32[8,128]{1,0:T(8,128)} %param.16), kind=kLoop, calls=%fused_computation.33 | loop fusion | flops 1024 | bytes 8192 | tf_op jit(solution)/shard_map/concatenate | solution.py:166
  4.7 3.5 %collective-permute-start = (f32[65,2,128]{2,1,0:T(2,128)S(1)}, f32[65,2,128]{2,1,0:T(2,128)S(1)}, u32[]{:S(2)}, u32[]{:S(2)}) collective-permute-start(f32[65,2,128]{2,1,0:T(2,128)S(1)} %get-tuple-element.150), channel_id=1, source_target_pairs={{0,8},{8,16},{16,24},{24,32},{32,40},{40,48},{48,56},{56,64},{64,7... | collective-permute-start | bytes 199688 | tf_op jit(solution)/shard_map/ppermute | solution.py:22
  8.2 7.8 %collective-permute-start.1 = (f32[65,2,128]{2,1,0:T(2,128)S(1)}, f32[65,2,128]{2,1,0:T(2,128)S(1)}, u32[]{:S(2)}, u32[]{:S(2)}) collective-permute-start(f32[65,2,128]{2,1,0:T(2,128)S(1)} %get-tuple-element.151), channel_id=1, source_target_pairs={{8,0},{16,8},{24,16},{32,24},{40,32},{48,40},{56,48},{64,56},{72,6... | collective-permute-start | bytes 199688 | tf_op jit(solution)/shard_map/ppermute | solution.py:25
  16.1 0.1 slice.759
  16.2 0.2 copy.21
  16.4 1.0 %stack.10 = f32[64,65,8,3]{1,2,3,0:T(8,128)} broadcast(f32[65,8,3]{0,1,2:T(8,128)S(1)} %copy.21), dimensions={1,2,3} | broadcast | bytes 405600 | tf_op jit(solution)/shard_map/stack | solution.py:196
  17.3 8.1 %all-to-all-start = ((f32[64,65,8,3]{1,2,3,0:T(8,128)}), f32[64,65,8,3]{1,2,3,0:T(8,128)S(1)}, u32[]{:S(2)}, u32[]{:S(2)}) async-start(f32[64,65,8,3]{1,2,3,0:T(8,128)} %stack.10), calls=%async_computation | async-start | bytes 1572864 | tf_op jit(solution)/shard_map/all_to_all | solution.py:196
  26.2 0.0 collective-permute-done
  26.2 0.0 collective-permute-done.1
  26.2 0.1 pad_maximum_fusion
  26.3 0.2 fusion.161
  26.5 0.2 copy.17
  26.7 0.2 copy.18
  27.0 1.9 %collective-permute-start.3 = (f32[65,12,2]{0,2,1:T(2,128)S(1)}, f32[65,12,2]{0,2,1:T(2,128)S(1)}, u32[]{:S(2)}, u32[]{:S(2)}) collective-permute-start(f32[65,12,2]{0,2,1:T(2,128)S(1)} %copy.18), channel_id=1, source_target_pairs={{1,0},{2,1},{3,2},{4,3},{5,4},{6,5},{7,6},{0,7},{9,8},{10,9},{11,1... | collective-permute-start | bytes 18728 | tf_op jit(solution)/shard_map/ppermute | solution.py:25
  28.9 2.4 %collective-permute-start.2 = (f32[65,12,2]{0,2,1:T(2,128)S(1)}, f32[65,12,2]{0,2,1:T(2,128)S(1)}, u32[]{:S(2)}, u32[]{:S(2)}) collective-permute-start(f32[65,12,2]{0,2,1:T(2,128)S(1)} %copy.17), channel_id=1, source_target_pairs={{0,1},{1,2},{2,3},{3,4},{4,5},{5,6},{6,7},{7,0},{8,9},{9,10},{10,1... | collective-permute-start | bytes 18728 | tf_op jit(solution)/shard_map/ppermute | solution.py:22
  31.3 3.5 %collective-permute-done.2 = f32[65,12,2]{0,2,1:T(2,128)S(1)} collective-permute-done((f32[65,12,2]{0,2,1:T(2,128)S(1)}, f32[65,12,2]{0,2,1:T(2,128)S(1)}, u32[]{:S(2)}, u32[]{:S(2)}) %collective-permute-start.2) | collective-permute-done | bytes 6272 | tf_op jit(solution)/shard_map/ppermute | solution.py:22
  34.8 0.3 copy.19
  35.2 0.0 collective-permute-done.3
  35.2 0.3 copy.20
  35.5 0.0 copy-start.3
  35.5 0.8 %maximum_multiply_fusion = f32[65,12,132]{2,1,0:T(8,128)S(1)} fusion(f32[65,12,2]{2,1,0:T(8,128)S(1)} %copy.20, f32[65,2,128]{2,1,0:T(2,128)S(1)} %collective-permute-done.1, f32[65,8,128]{2,1,0:T(8,128)S(1)} %constant_dynamic-update-slice_fusion, f32[65,2,128]{2,1,0:T(2,128)S(1)} %collective-permute-done, f32[65,12,2]{2,1,0:T(8,128)S(1)} %copy.19, ...), kind=kLoop, calls=%fused_computation.2 | loop fusion | flops 514800 | bytes 824208 | tf_op jit(solution)/shard_map/mul | solution.py:207
  36.3 12.8 %all-to-all-done = f32[64,65,8,3]{1,2,3,0:T(8,128)S(1)} async-done(((f32[64,65,8,3]{1,2,3,0:T(8,128)}), f32[64,65,8,3]{1,2,3,0:T(8,128)S(1)}, u32[]{:S(2)}, u32[]{:S(2)}) %all-to-all-start) | async-done | bytes 399392 | tf_op jit(solution)/shard_map/all_to_all | solution.py:196
  49.1 0.5 convolution_bitcast_fusion
  49.6 0.0 copy-done.3
  49.6 0.3 copy.24
  50.0 0.3 maximum_select_fusion
  50.3 0.0 copy-start
  50.3 0.1 compare_select_fusion
  50.4 0.2 reduce-window_subtract_fusion
  50.5 0.0 copy-start.1
  50.6 0.2 multiply_multiply_fusion.3
  50.8 0.7 %copy-done.1 = f32[15,8,128]{2,1,0:T(8,128)S(1)} copy-done((f32[15,8,128]{2,1,0:T(8,128)S(1)}, f32[15,8,128]{2,1,0:T(8,128)}, u32[]{:S(2)}) %copy-start.1) | copy-done | bytes 61464
  51.4 0.1 slice_multiply_fusion.10
  51.7 0.4 fusion.29
  52.1 0.0 copy-start.2
  52.1 0.0 copy-done
  52.1 0.4 fusion.42
  52.5 0.0 slice-start
  52.6 0.2 copy-done.2
  52.8 0.1 fusion.89
  52.9 0.1 constant_dynamic-update-slice_fusion.36
  53.2 0.0 copy-start.4
  53.2 0.1 fusion.72
  53.3 0.1 constant_dynamic-update-slice_fusion.52
  53.6 0.0 copy-start.5
  53.7 0.0 slice-done
  53.7 0.3 fusion.11
  54.0 0.0 copy-done.4
  54.0 0.2 copy-done.5
  54.2 0.1 constant_dynamic-update-slice_fusion.20
  54.5 0.7 %slice_bitcast_fusion = (f32[16,8,128]{2,1,0:T(8,128)}, f32[16,8,128]{2,1,0:T(8,128)}) fusion(f32[2,16,8,128]{3,2,1,0:T(8,128)S(1)} %constant_dynamic-update-slice_fusion.5), kind=kLoop, calls=%fused_computation.126 | loop fusion | bytes 262144 | tf_op jit(solution)/shard_map/squeeze | solution.py:150
  (63 shorter events, 0.5 us)
Async XLA Ops:
  4.7 21.4 %collective-permute-start = (f32[65,2,128]{2,1,0:T(2,128)S(1)}, f32[65,2,128]{2,1,0:T(2,128)S(1)}, u32[]{:S(2)}, u32[]{:S(2)}) collective-permute-start(f32[65,2,128]{2,1,0:T(2,128)S(1)} %get-tuple-element.150), channel_id=1, source_target_pairs={{0,8},{8,16},{16,24},{24,32},{32,40},{40,48},{48,56},{56,64},{64,7... | collective-permute-start | bytes 199688 | tf_op jit(solution)/shard_map/ppermute | solution.py:22
  8.2 17.9 %collective-permute-start.1 = (f32[65,2,128]{2,1,0:T(2,128)S(1)}, f32[65,2,128]{2,1,0:T(2,128)S(1)}, u32[]{:S(2)}, u32[]{:S(2)}) collective-permute-start(f32[65,2,128]{2,1,0:T(2,128)S(1)} %get-tuple-element.151), channel_id=1, source_target_pairs={{8,0},{16,8},{24,16},{32,24},{40,32},{48,40},{56,48},{64,56},{72,6... | collective-permute-start | bytes 199688 | tf_op jit(solution)/shard_map/ppermute | solution.py:25
  17.3 31.8 %all-to-all-start = ((f32[64,65,8,3]{1,2,3,0:T(8,128)}), f32[64,65,8,3]{1,2,3,0:T(8,128)S(1)}, u32[]{:S(2)}, u32[]{:S(2)}) async-start(f32[64,65,8,3]{1,2,3,0:T(8,128)} %stack.10), calls=%async_computation | async-start | bytes 1572864 | tf_op jit(solution)/shard_map/all_to_all | solution.py:196
  27.0 8.2 %collective-permute-start.3 = (f32[65,12,2]{0,2,1:T(2,128)S(1)}, f32[65,12,2]{0,2,1:T(2,128)S(1)}, u32[]{:S(2)}, u32[]{:S(2)}) collective-permute-start(f32[65,12,2]{0,2,1:T(2,128)S(1)} %copy.18), channel_id=1, source_target_pairs={{1,0},{2,1},{3,2},{4,3},{5,4},{6,5},{7,6},{0,7},{9,8},{10,9},{11,1... | collective-permute-start | bytes 18728 | tf_op jit(solution)/shard_map/ppermute | solution.py:25
  28.9 5.9 %collective-permute-start.2 = (f32[65,12,2]{0,2,1:T(2,128)S(1)}, f32[65,12,2]{0,2,1:T(2,128)S(1)}, u32[]{:S(2)}, u32[]{:S(2)}) collective-permute-start(f32[65,12,2]{0,2,1:T(2,128)S(1)} %copy.17), channel_id=1, source_target_pairs={{0,1},{1,2},{2,3},{3,4},{4,5},{5,6},{6,7},{7,0},{8,9},{9,10},{10,1... | collective-permute-start | bytes 18728 | tf_op jit(solution)/shard_map/ppermute | solution.py:22
  35.5 14.1 %copy-start.3 = (f32[65]{0:T(128)S(1)}, f32[65]{0:T(128)}, u32[]{:S(2)}) copy-start(f32[65]{0:T(128)} %constant.125.clone.1) | copy-start | bytes 784
  50.3 1.9 %copy-start = (f32[65,12,132]{2,1,0:T(8,128)}, f32[65,12,132]{2,1,0:T(8,128)S(1)}, u32[]{:S(2)}) copy-start(f32[65,12,132]{2,1,0:T(8,128)S(1)} %maximum_select_fusion) | copy-start | bytes 1235524
  50.5 0.9 %copy-start.1 = (f32[15,8,128]{2,1,0:T(8,128)S(1)}, f32[15,8,128]{2,1,0:T(8,128)}, u32[]{:S(2)}) copy-start(f32[15,8,128]{2,1,0:T(8,128)} %param.18) | copy-start | bytes 184324
  52.1 0.7 %copy-start.2 = (f32[2,8,128]{2,1,0:T(8,128)S(1)}, f32[2,8,128]{2,1,0:T(8,128)}, u32[]{:S(2)}) copy-start(f32[2,8,128]{2,1,0:T(8,128)} %param.19) | copy-start | bytes 24580
  52.5 1.1 %slice-start = ((f32[65,12,132]{2,1,0:T(8,128)}), f32[32,12,132]{2,1,0:T(8,128)S(1)}, s32[]{:S(2)}) async-start(f32[65,12,132]{2,1,0:T(8,128)} %copy-done), calls=%async_computation.1 | async-start | bytes 1048576 | tf_op jit(solution)/shard_map/slice | solution.py:66
  53.2 0.8 %copy-start.4 = (f32[16,8,128]{2,1,0:T(8,128)}, f32[16,8,128]{2,1,0:T(8,128)S(1)}, u32[]{:S(2)}) copy-start(f32[16,8,128]{2,1,0:T(8,128)S(1)} %constant_dynamic-update-slice_fusion.21) | copy-start | bytes 196612
  53.6 0.6 %copy-start.5 = (f32[16,8,128]{2,1,0:T(8,128)}, f32[16,8,128]{2,1,0:T(8,128)S(1)}, u32[]{:S(2)}) copy-start(f32[16,8,128]{2,1,0:T(8,128)S(1)} %constant_dynamic-update-slice_fusion.37) | copy-start | bytes 196612
